TPU v7x, 128 devices: a whole 4x4x4 slice. The times are simulated.
128 devices in a mesh: site: 32 (over z, y, core), branch: 4 (over x).
Axes of the slice: x: 4, y: 4, z: 4, core: 2. Of those that a mesh axis runs over, the one named last changes fastest.
Arguments:
- states: int32 [256, 8192], P(None, 'site'), may hold values from 0 to 63, as said below
- gap_mask: int32 [256, 8192], P(None, 'site'), may hold values 0 or 1
- weights: int32 [8192], P('site'), may hold values from 1 to 9
- leaf_order: int32 [256], replicated, may hold values from 0 to 255, each once
- exchanges: float32 [64, 64], replicated, may hold values from 0.3 to 3
- codon_freq: float32 [64], replicated, may hold values from 0.3 to 3
- omega_ratio: float32 [8], replicated, may hold values from 0.1 to 2
- lengths: float32 [508], P('branch'), may hold values from 0.05 to 1.5
- classes: int32 [508], P('branch'), may hold values from 0 to 7
Outputs:
- grad_exch: float32 [64, 64], replicated
- grad_omega: float32 [8], replicated
- grad_length: float32 [508], P('branch')
- loglik: float32 [], replicated
Inputs may be any that keep to these rules, and one draw needn't show every extreme that they name: `states`: every state is a sense codon: never 10, 11 or 14.
All inputs are finite; a program needn't handle non-finite values. No bound on the sum of `gap_mask` on one device may be relied on, other than what follows from the above.
Results may differ from a plain program's by a relative error of at most 0.0003.
Values sent between devices are 32-bit elements; how exact they have to be, the bound alone decides.
A program may use at most 192 MiB of HBM per device.

v0:
```python
import jax
import jax.numpy as jnp
import numpy as np
from jax import lax
from jax.sharding import PartitionSpec as P

LEVELS = 6
LEAF_DEV = 64
EDGES = 127
SLOTS = 128
CLASSES = 8
CODE_TABLE = "FFLLSSSSYYXXCCXWLLLLPPPPHHQQRRRRIIIMTTTTNNKKSSRRVVVVAAAADDEEGGGG"


def codon_tables():
    amino_acid = np.array(list(CODE_TABLE))
    codon_index = np.arange(64)
    digits = np.stack([codon_index // 16, codon_index // 4 % 4, codon_index % 4], 1)
    differ = (digits[:, None, :] != digits[None, :, :]).sum(-1)
    is_sense = amino_acid != "X"
    single = (differ == 1) & is_sense[:, None] & is_sense[None, :]
    nonsyn = single & (amino_acid[:, None] != amino_acid[None, :])
    return (is_sense.astype(np.float32), single.astype(np.float32), nonsyn.astype(np.float32))


def build_rates(exchanges, codon_freq, omega_ratio):
    is_sense, single, nonsyn = codon_tables()
    stationary = codon_freq * is_sense / jnp.sum(codon_freq * is_sense)
    symmetric = 0.5 * (exchanges + exchanges.T)
    factor = 1.0 + nonsyn[None, :, :] * (omega_ratio[:, None, None] - 1.0)
    off_diag = symmetric[None, :, :] * stationary[None, None, :] * factor * single[None, :, :]
    row_total = jnp.sum(off_diag, axis=2)
    mean_rate = jnp.sum(stationary[None, :] * row_total, axis=1)
    identity = jnp.eye(64, dtype=exchanges.dtype)
    rate_matrix = (off_diag - row_total[:, :, None] * identity[None]) / mean_rate[:, None, None]
    return (rate_matrix, stationary)


def product(left, right):
    return jnp.einsum("bij,bjk->bik", left, right, precision=lax.Precision.HIGHEST)


def expm_taylor(scaled):
    reduced = scaled / 16.0
    identity = jnp.eye(64, dtype=scaled.dtype)
    series = jnp.broadcast_to(identity, scaled.shape)
    for degree in range(8, 0, -1):
        series = identity + product(reduced, series) / degree
    for square_step in range(4):
        series = product(series, series)
    return series


def forward(probs, vectors):
    return jnp.einsum("bij,bjs->bis", probs, vectors, precision=lax.Precision.HIGHEST)


def carried(probs, vectors):
    return jnp.einsum("bji,bjs->bis", probs, vectors, precision=lax.Precision.HIGHEST)


def leaf_partials(leaf_states, gap_rows):
    codon_axis = jnp.arange(64, dtype=jnp.int32)
    indicator = (leaf_states[:, None, :] == codon_axis[None, :, None]).astype(jnp.float32)
    return jnp.where(gap_rows[:, None, :] > 0, jnp.float32(1.0), indicator)


def up_pass(probs, leaves):
    levels = [leaves]
    messages = []
    logscale = jnp.zeros(leaves.shape[2:], jnp.float32)
    current = leaves
    for height in range(LEVELS):
        amount = current.shape[0]
        offset = 2 * LEAF_DEV - 2 * amount
        message = forward(probs[offset : offset + amount], current)
        messages.append(message)
        raw_parent = message[0::2] * message[1::2]
        scaling = jnp.sum(raw_parent, axis=1)
        current = raw_parent / scaling[:, None, :]
        logscale = logscale + jnp.sum(jnp.log(scaling), axis=0)
        levels.append(current)
    messages.append(forward(probs[EDGES - 1 : EDGES], current))
    return (levels, messages, logscale)


def root_terms(stationary, top_messages, top_logs):
    members = top_messages.shape[0]
    joint = stationary[:, None] * top_messages[0]
    for member in range(1, members):
        joint = joint * top_messages[member]
    site_ll = jnp.log(jnp.sum(joint, axis=0)) + jnp.sum(top_logs, axis=0)
    above_list = []
    for member in range(members):
        vector = jnp.broadcast_to(stationary[:, None], top_messages.shape[1:])
        for other in range(members):
            if other != member:
                vector = vector * top_messages[other]
        above_list.append(vector)
    return (site_ll, jnp.stack(above_list))


def down_pass(probs, levels, messages, above_top):
    a_list = [above_top]
    current = above_top
    for height in range(LEVELS, 0, -1):
        amount = levels[height].shape[0]
        offset = 2 * LEAF_DEV - 2 * amount
        down_part = carried(probs[offset : offset + amount], current)
        down_part = down_part / jnp.sum(down_part, axis=1, keepdims=True)
        message = messages[height - 1]
        current = jnp.stack([down_part * message[1::2], down_part * message[0::2]], axis=1).reshape(
            message.shape
        )
        a_list.append(current)
    return a_list[::-1]


def weigh(a_list, messages, site_weight, total_sites):
    weighted = []
    for vector, message in zip(a_list, messages):
        likelihood = jnp.sum(vector * message, axis=1)
        weighted.append(vector * (site_weight / (likelihood * total_sites))[:, None, :])
    return weighted


def body(
    states, gap_mask, weights, leaf_order, exchanges, codon_freq, omega_ratio, lengths, classes
):
    site_count = lax.axis_size("site")
    site_pos = lax.axis_index("site")
    subtree = lax.axis_index("branch")
    site_span = states.shape[1]
    total_sites = site_span * site_count
    total_taxa = LEAF_DEV * lax.axis_size("branch")
    rate_matrix, stationary = build_rates(exchanges, codon_freq, omega_ratio)
    slot_len = jnp.concatenate([lengths, jnp.zeros((1,), lengths.dtype)])
    slot_cls = jnp.concatenate([classes, jnp.zeros((1,), jnp.int32)])
    class_pick = (slot_cls[:, None] == jnp.arange(CLASSES, dtype=jnp.int32)[None, :]).astype(
        jnp.float32
    )
    slot_rates = jnp.einsum("bc,cij->bij", class_pick, rate_matrix, precision=lax.Precision.HIGHEST)
    scaled = slot_rates * slot_len[:, None, None]
    per_dev = SLOTS // site_count
    own_start = site_pos * per_dev
    own_scaled = lax.dynamic_slice_in_dim(scaled, own_start, per_dev, 0)
    own_pull = None
    own_probs, own_pull = jax.vjp(expm_taylor, own_scaled)
    probs = lax.all_gather(own_probs, "site", axis=0, tiled=True)
    taxon_rows = lax.dynamic_slice_in_dim(leaf_order, subtree * LEAF_DEV, LEAF_DEV, 0)
    leaves = leaf_partials(
        jnp.take(states, taxon_rows, axis=0), jnp.take(gap_mask, taxon_rows, axis=0)
    )
    levels, messages, logscale = up_pass(probs, leaves)
    top_messages, top_logs = (
        lax.all_gather(messages[-1], "branch", axis=0, tiled=True),
        lax.all_gather(logscale[None, :], "branch", axis=0, tiled=True),
    )
    site_ll, above_all = root_terms(stationary, top_messages, top_logs)
    site_weight = weights.astype(jnp.float32)
    loglik_part = jnp.sum(site_weight * site_ll)
    log_total = lax.psum(loglik_part, "site")
    above_top = lax.dynamic_slice_in_dim(above_all, subtree, 1, 0)
    a_list = down_pass(probs, levels, messages, above_top)
    weighted = weigh(a_list, messages, site_weight, total_sites)
    padding = jnp.zeros((1, 64, site_span), jnp.float32)
    weighted_all = jnp.concatenate(weighted + [padding], axis=0)
    partial_all = jnp.concatenate(levels + [padding], axis=0)
    part_above = lax.slice_in_dim(weighted_all, 0, lax.axis_size("site") * per_dev, axis=0)
    part_below = lax.slice_in_dim(partial_all, 0, lax.axis_size("site") * per_dev, axis=0)
    own_counts = lax.psum_scatter(
        jnp.einsum("bis,bjs->bij", part_above, part_below, precision=lax.Precision.HIGHEST),
        "site",
        scatter_dimension=0,
        tiled=True,
    )
    d_scaled = own_pull(own_counts)[0]
    use_rates = lax.dynamic_slice_in_dim(slot_rates, own_start, per_dev, 0)
    use_len = lax.dynamic_slice_in_dim(slot_len, own_start, per_dev, 0)
    use_pick = lax.dynamic_slice_in_dim(class_pick, own_start, per_dev, 0)
    d_length = jnp.sum(d_scaled * use_rates, axis=(1, 2))
    d_rates = jnp.einsum(
        "bc,bij->cij", use_pick, d_scaled * use_len[:, None, None], precision=lax.Precision.HIGHEST
    )
    unused_rates, pull_rates = jax.vjp(
        lambda table, ratio: build_rates(table, codon_freq, ratio)[0], exchanges, omega_ratio
    )
    d_exch, d_omega = pull_rates(d_rates)
    grad_exch, grad_omega = lax.psum((d_exch, d_omega), ("site", "branch"))
    loglik = log_total / total_sites / total_taxa
    length_out = lax.all_gather(d_length, "site", axis=0, tiled=True)[:EDGES]
    return (grad_exch, grad_omega, length_out, loglik)


def solution(mesh):
    return jax.shard_map(
        body,
        mesh=mesh,
        in_specs=(
            P(None, "site"),
            P(None, "site"),
            P("site"),
            P(),
            P(),
            P(),
            P(),
            P("branch"),
            P("branch"),
        ),
        out_specs=(P(), P(), P("branch"), P()),
        check_vma=False,
    )
```

profile of v0, /device:TPU:1, one launch (start us, length us, event | category | flops | bytes accessed | tf_op | source)
XLA Modules:
  0.0 396.8 jit_solution(4793267185517987480)
XLA Ops:
  7.3 0.7 broadcast_add_fusion
  7.9 0.8 copy.99
  8.8 0.7 pad_add_fusion
  9.5 0.7 pad_maximum_fusion.5
  10.8 1.3 fusion.76
  12.8 0.8 fusion.61
  13.5 1.0 fusion.29
  14.7 2.7 fusion.27
  18.1 0.7 copy.144
  23.1 0.7 copy-done.14
  25.6 0.9 fusion.81
  27.8 0.7 gather_fusion.1
  28.4 0.7 gather_fusion
  29.3 2.9 convert_select_fusion.4
  32.2 2.7 fusion.6
  34.8 41.9 %all-gather.5.cloned.1.call-done = f32[128,64,64]{2,1,0:T(8,128)} async-done(((f32[4,64,64]{2,1,0:T(8,128)}), f32[128,64,64]{2,1,0:T(8,128)}) %all-gather.5.cloned.1.call-update) | async-done | bytes 2097168 | tf_op jit(solution)/shard_map/all_gather | solution.py:149
  76.7 6.6 %fusion.7 = f32[64,64,256]{2,1,0:T(8,128)S(1)} fusion(f32[128,64,64]{2,1,0:T(8,128)} %all-gather.5.cloned.1.call-done, f32[64,64,256]{2,1,0:T(8,128)} %convert_select_fusion.4), kind=kOutput, calls=%fused_computation.13 | convolution fusion | flops 805306368 | bytes 10485760 | tf_op jit(solution)/shard_map/bij,bjs->bis/dot_general | solution.py:55
  83.8 1.7 copy-done.2
  85.5 2.1 fusion.24
  87.7 1.1 fusion.26
  91.0 10.3 %all-gather = f32[256,256]{1,0:T(8,128)S(1)} all-gather(f32[64,256]{1,0:T(8,128)S(1)} %fusion.53), channel_id=2, replica_groups=mesh['site'=32,'branch'=4] {'branch'}, dimensions={0}, use_global_device_ids=true | all-gather | bytes 327680 | tf_op jit(solution)/shard_map/all_gather | solution.py:156
  102.0 7.3 %all-gather.2 = f32[4,1,256]{2,1,0:T(1,128)} all-gather(f32[1,1,256]{2,1,0:T(1,128)S(1)} %bitcast.204), channel_id=3, replica_groups=mesh['site'=32,'branch'=4] {'branch'}, dimensions={0}, use_global_device_ids=true | all-gather | bytes 5120 | tf_op jit(solution)/shard_map/all_gather | solution.py:157
  113.5 0.7 multiply_divide_fusion.3
  114.2 0.7 fusion.89
  116.0 0.8 multiply_divide_fusion.2
  116.8 1.1 fusion.90
  117.9 1.0 fusion.12
  120.2 2.0 fusion.91
  122.2 1.9 fusion.11
  124.7 2.4 multiply_bitcast_fusion.1
  127.7 1.4 fusion.5
  129.1 3.4 constant_dynamic-update-slice_fusion.1
  132.5 1.2 reduce_sum.398
  133.8 3.3 multiply_dynamic-update-slice_fusion
  137.2 1.1 multiply_dynamic-update-slice_fusion.1
  138.3 0.8 multiply_dynamic-update-slice_fusion.2
  139.1 0.7 multiply_dynamic-update-slice_fusion.3
  140.5 0.7 multiply_reduce_fusion.12
  142.5 1.2 fusion.25
  143.6 0.9 fusion.30
  144.5 0.7 fusion.42
  145.3 0.7 fusion.58
  147.2 15.7 %fusion.82 = f32[128,64,64]{2,1,0:T(8,128)} fusion(f32[128,64,256]{2,1,0:T(8,128)} %constant_dynamic-update-slice_fusion, f32[128,64,256]{2,1,0:T(8,128)} %constant_dynamic-update-slice_fusion.2), kind=kOutput, calls=%fused_computation.221 | convolution fusion | flops 1610612736 | bytes 18874368 | tf_op jit(solution)/shard_map/bis,bjs->bij/dot_general | solution.py:172
  164.9 80.7 %reduce-scatter.2.cloned.1.call-done = f32[4,64,64]{2,1,0:T(8,128)} async-done(((f32[128,64,64]{2,1,0:T(8,128)}), f32[4,64,64]{2,1,0:T(8,128)}) %reduce-scatter.2.cloned.1.call-update) | async-done | bytes 65552 | tf_op jit(solution)/shard_map/reduce_scatter | solution.py:171
  245.6 1.3 fusion.83
  246.9 1.2 convolution_add_fusion.10
  258.5 64.8 %all-reduce.2 = (f32[128]{0:T(128)}, f32[]{:T(128)}) all-reduce(f32[128]{0:T(128)S(1)} %dynamic-update-slice, f32[]{:T(128)} %get-tuple-element.42), channel_id=1, replica_groups=mesh['site'=32,'branch'=4] {'site'}, use_global_device_ids=true, to_apply=%add | all-reduce | flops 129 | bytes 1032
  323.9 64.7 %all-reduce.1 = (f32[64,64]{1,0:T(8,128)}, f32[8]{0:T(128)}) all-reduce(f32[64,64]{1,0:T(8,128)S(1)} %fusion.60, f32[8]{0:T(128)S(1)} %get-tuple-element.5), channel_id=1, replica_groups=mesh['site'=32,'branch'=4] {'site','branch'}, use_global_device_ids=true, to_apply=%region_29.31 | all-reduce | flops 4104 | bytes 32832 | tf_op jit(solution)/shard_map/psum | solution.py:189
  (276 shorter events, 34.8 us)
Async XLA Ops:
  7.2 20.6 %copy-start = (s32[256,256]{1,0:T(8,128)S(1)}, s32[256,256]{1,0:T(8,128)}, u32[]{:S(2)}) copy-start(s32[256,256]{1,0:T(8,128)} %param.17) | copy-start | bytes 786436
  7.2 69.5 %all-gather.5.cloned.1.call-start = ((), (), s32[]{:S(2)}) async-start(), calls=%async_computation.1 | async-start | bytes 4325376 | tf_op jit(solution)/shard_map/all_gather | solution.py:149
  7.2 13.9 %copy-start.12 = (f32[64,64]{1,0:T(8,128)}, f32[64,64]{1,0:T(8,128)S(1)}, u32[]{:S(2)}) copy-start(f32[64,64]{1,0:T(8,128)S(1)} %fusion.62) | copy-start | bytes 49156
  7.9 9.5 %copy-start.69 = (f32[8]{0:T(128)}, f32[8]{0:T(128)S(1)}, u32[]{:S(2)}) copy-start(f32[8]{0:T(128)S(1)} %broadcast_add_fusion) | copy-start | bytes 100
  9.5 7.9 %copy-start.78 = (s32[128]{0:T(128)}, s32[128]{0:T(128)S(1)}, u32[]{:S(2)}) copy-start(s32[128]{0:T(128)S(1)} %pad_add_fusion) | copy-start | bytes 1540
  10.8 10.3 %copy-start.51 = (f32[4]{0:T(128)}, f32[4]{0:T(128)S(1)}, u32[]{:S(2)}) copy-start(f32[4]{0:T(128)S(1)} %get-tuple-element.14) | copy-start | bytes 52
  18.0 9.0 %copy-start.75 = (s32[256]{0:T(256)S(1)}, s32[256]{0:T(256)}, u32[]{:S(2)}) copy-start(s32[256]{0:T(256)} %param.19) | copy-start | bytes 3076
  18.1 9.6 %copy-start.81 = (s32[256]{0:T(256)S(1)}, s32[256]{0:T(256)}, u32[]{:S(2)}) copy-start(s32[256]{0:T(256)} %param.20) | copy-start | bytes 3076
  18.1 10.4 %copy-start.38 = (s32[256,256]{1,0:T(8,128)S(1)}, s32[256,256]{1,0:T(8,128)}, u32[]{:S(2)}) copy-start(s32[256,256]{1,0:T(8,128)} %param.18) | copy-start | bytes 786436
  26.5 219.1 %reduce-scatter.2.cloned.1.call-start = ((), (), s32[]{:S(2)}) async-start(), calls=%async_computation.2 | async-start | bytes 4325376 | tf_op jit(solution)/shard_map/reduce_scatter | solution.py:171
  88.8 12.4 %copy-start.61 = (f32[64]{0:T(128)S(1)}, f32[64]{0:T(128)}, u32[]{:S(2)}) copy-start(f32[64]{0:T(128)} %copy-done.60) | copy-start | bytes 772
  89.6 23.8 %copy-start.8 = (f32[8,64,256]{2,1,0:T(8,128)}, f32[8,64,256]{2,1,0:T(8,128)S(1)}, u32[]{:S(2)}) copy-start(f32[8,64,256]{2,1,0:T(8,128)S(1)} %fusion.31) | copy-start | bytes 1572868
  89.6 21.8 %copy-start.56 = (f32[256]{0:T(256)S(1)}, f32[256]{0:T(256)}, u32[]{:S(2)}) copy-start(f32[256]{0:T(256)} %convert_element_type.42) | copy-start | bytes 3076
  90.1 21.2 %copy-start.10 = (f32[4,64,256]{2,1,0:T(8,128)}, f32[4,64,256]{2,1,0:T(8,128)S(1)}, u32[]{:S(2)}) copy-start(f32[4,64,256]{2,1,0:T(8,128)S(1)} %fusion.43) | copy-start | bytes 786436
  90.4 20.9 %copy-start.22 = (f32[2,64,256]{2,1,0:T(8,128)}, f32[2,64,256]{2,1,0:T(8,128)S(1)}, u32[]{:S(2)}) copy-start(f32[2,64,256]{2,1,0:T(8,128)S(1)} %fusion.59) | copy-start | bytes 393220
  90.8 20.2 %copy-start.66 = (f32[256]{0:T(256)}, f32[256]{0:T(256)S(1)}, u32[]{:S(2)}) copy-start(f32[256]{0:T(256)S(1)} %fusion.69) | copy-start | bytes 3076
  133.8 6.7 %copy-start.73 = (f32[256]{0:T(256)S(1)}, f32[256]{0:T(256)}, u32[]{:S(2)}) copy-start(f32[256]{0:T(256)} %multiply_reduce_fusion.10) | copy-start | bytes 3076
  133.8 6.7 %copy-start.74 = (f32[256]{0:T(256)S(1)}, f32[256]{0:T(256)}, u32[]{:S(2)}) copy-start(f32[256]{0:T(256)} %get-tuple-element.15) | copy-start | bytes 3076
  133.8 6.7 %copy-start.76 = (s32[256]{0:T(256)S(1)}, s32[256]{0:T(256)}, u32[]{:S(2)}) copy-start(s32[256]{0:T(256)} %param.19) | copy-start | bytes 3076
  133.8 6.7 %copy-start.77 = (f32[256]{0:T(256)S(1)}, f32[256]{0:T(256)}, u32[]{:S(2)}) copy-start(f32[256]{0:T(256)} %reduce_sum.398) | copy-start | bytes 3076
  133.8 7.4 %copy-start.44 = (f32[1,64,256]{2,1,0:T(8,128)S(1)}, f32[1,64,256]{2,1,0:T(8,128)}, u32[]{:S(2)}) copy-start(f32[1,64,256]{2,1,0:T(8,128)} %copy-done.43) | copy-start | bytes 196612
  137.2 7.3 %copy-start.9 = (f32[8,64,256]{2,1,0:T(8,128)S(1)}, f32[8,64,256]{2,1,0:T(8,128)}, u32[]{:S(2)}) copy-start(f32[8,64,256]{2,1,0:T(8,128)} %copy-done.8) | copy-start | bytes 1572868
  137.2 7.3 %copy-start.58 = (f32[4,256]{1,0:T(4,128)S(1)}, f32[4,256]{1,0:T(4,128)}, u32[]{:S(2)}) copy-start(f32[4,256]{1,0:T(4,128)} %copy-done.57) | copy-start | bytes 12292
  138.3 7.0 %copy-start.11 = (f32[4,64,256]{2,1,0:T(8,128)S(1)}, f32[4,64,256]{2,1,0:T(8,128)}, u32[]{:S(2)}) copy-start(f32[4,64,256]{2,1,0:T(8,128)} %copy-done.10) | copy-start | bytes 786436
  138.3 7.0 %copy-start.64 = (f32[2,256]{1,0:T(2,128)S(1)}, f32[2,256]{1,0:T(2,128)}, u32[]{:S(2)}) copy-start(f32[2,256]{1,0:T(2,128)} %copy-done.63) | copy-start | bytes 6148
  138.3 7.6 %copy-start.23 = (f32[2,64,256]{2,1,0:T(8,128)S(1)}, f32[2,64,256]{2,1,0:T(8,128)}, u32[]{:S(2)}) copy-start(f32[2,64,256]{2,1,0:T(8,128)} %copy-done.22) | copy-start | bytes 393220
  138.3 7.6 %copy-start.67 = (f32[256]{0:T(256)S(1)}, f32[256]{0:T(256)}, u32[]{:S(2)}) copy-start(f32[256]{0:T(256)} %copy-done.66) | copy-start | bytes 3076
  162.9 82.7 %copy-start.19 = (f32[4,64,64]{2,1,0:T(8,128)S(1)}, f32[4,64,64]{2,1,0:T(8,128)}, u32[]{:S(2)}) copy-start(f32[4,64,64]{2,1,0:T(8,128)} %copy-done.18) | copy-start | bytes 196612
  162.9 85.3 %copy-start.17 = (f32[4,64,64]{2,1,0:T(8,128)S(1)}, f32[4,64,64]{2,1,0:T(8,128)}, u32[]{:S(2)}) copy-start(f32[4,64,64]{2,1,0:T(8,128)} %copy-done.16) | copy-start | bytes 196612
  162.9 86.0 %copy-start.15 = (f32[4,64,64]{2,1,0:T(8,128)S(1)}, f32[4,64,64]{2,1,0:T(8,128)}, u32[]{:S(2)}) copy-start(f32[4,64,64]{2,1,0:T(8,128)} %copy-done.14) | copy-start | bytes 196612
  162.9 86.8 %copy-start.21 = (f32[4,64,64]{2,1,0:T(8,128)S(1)}, f32[4,64,64]{2,1,0:T(8,128)}, u32[]{:S(2)}) copy-start(f32[4,64,64]{2,1,0:T(8,128)} %copy-done.20) | copy-start | bytes 196612
  162.9 87.8 %copy-start.25 = (f32[4,64,64]{2,1,0:T(8,128)S(1)}, f32[4,64,64]{2,1,0:T(8,128)}, u32[]{:S(2)}) copy-start(f32[4,64,64]{2,1,0:T(8,128)} %copy-done.24) | copy-start | bytes 196612
  162.9 88.1 %copy-start.52 = (f32[4]{0:T(128)S(1)}, f32[4]{0:T(128)}, u32[]{:S(2)}) copy-start(f32[4]{0:T(128)} %copy-done.51) | copy-start | bytes 52
  162.9 89.1 %copy-start.37 = (f32[4,64,64]{2,1,0:T(8,128)S(1)}, f32[4,64,64]{2,1,0:T(8,128)}, u32[]{:S(2)}) copy-start(f32[4,64,64]{2,1,0:T(8,128)} %copy-done.36) | copy-start | bytes 196612
  162.9 89.9 %copy-start.35 = (f32[4,64,64]{2,1,0:T(8,128)S(1)}, f32[4,64,64]{2,1,0:T(8,128)}, u32[]{:S(2)}) copy-start(f32[4,64,64]{2,1,0:T(8,128)} %copy-done.34) | copy-start | bytes 196612
  163.0 90.7 %copy-start.33 = (f32[4,64,64]{2,1,0:T(8,128)S(1)}, f32[4,64,64]{2,1,0:T(8,128)}, u32[]{:S(2)}) copy-start(f32[4,64,64]{2,1,0:T(8,128)} %copy-done.32) | copy-start | bytes 196612
  163.0 91.5 %copy-start.31 = (f32[4,64,64]{2,1,0:T(8,128)S(1)}, f32[4,64,64]{2,1,0:T(8,128)}, u32[]{:S(2)}) copy-start(f32[4,64,64]{2,1,0:T(8,128)} %copy-done.30) | copy-start | bytes 196612
  164.9 90.4 %copy-start.29 = (f32[4,64,64]{2,1,0:T(8,128)S(1)}, f32[4,64,64]{2,1,0:T(8,128)}, u32[]{:S(2)}) copy-start(f32[4,64,64]{2,1,0:T(8,128)} %copy-done.28) | copy-start | bytes 196612
  248.1 8.0 %copy-start.27 = (f32[4,64,64]{2,1,0:T(8,128)S(1)}, f32[4,64,64]{2,1,0:T(8,128)}, u32[]{:S(2)}) copy-start(f32[4,64,64]{2,1,0:T(8,128)} %copy-done.26) | copy-start | bytes 196612
  248.9 7.6 %copy-start.13 = (f32[64,64]{1,0:T(8,128)S(1)}, f32[64,64]{1,0:T(8,128)}, u32[]{:S(2)}) copy-start(f32[64,64]{1,0:T(8,128)} %copy-done.12) | copy-start | bytes 49156
  248.9 7.6 %copy-start.80 = (f32[4]{0:T(128)S(1)}, f32[4]{0:T(128)}, u32[]{:S(2)}) copy-start(f32[4]{0:T(128)} %get-tuple-element.13) | copy-start | bytes 52
  249.3 7.7 %copy-start.46 = (f32[64,64]{1,0:T(8,128)S(1)}, f32[64,64]{1,0:T(8,128)}, u32[]{:S(2)}) copy-start(f32[64,64]{1,0:T(8,128)} %copy-done.45) | copy-start | bytes 49156
  249.3 7.7 %copy-start.48 = (f32[8,64]{0,1:T(8,128)S(1)}, f32[8,64]{0,1:T(8,128)}, u32[]{:S(2)}) copy-start(f32[8,64]{0,1:T(8,128)} %copy-done.47) | copy-start | bytes 6148
  249.3 7.7 %copy-start.49 = (f32[64,64]{1,0:T(8,128)S(1)}, f32[64,64]{1,0:T(8,128)}, u32[]{:S(2)}) copy-start(f32[64,64]{1,0:T(8,128)} %constant.103) | copy-start | bytes 49156
  249.4 7.7 %copy-start.50 = (f32[64,64]{1,0:T(8,128)S(1)}, f32[64,64]{1,0:T(8,128)}, u32[]{:S(2)}) copy-start(f32[64,64]{1,0:T(8,128)} %constant.102) | copy-start | bytes 49156
  249.4 7.7 %copy-start.70 = (f32[8]{0:T(128)S(1)}, f32[8]{0:T(128)}, u32[]{:S(2)}) copy-start(f32[8]{0:T(128)} %copy-done.69) | copy-start | bytes 100
  251.1 6.6 %copy-start.62 = (f32[64]{0:T(128)S(1)}, f32[64]{0:T(128)}, u32[]{:S(2)}) copy-start(f32[64]{0:T(128)} %copy-done.60) | copy-start | bytes 772
  251.6 137.0 %copy-start.1 = (s32[256,256]{1,0:T(8,128)S(1)}, s32[256,256]{1,0:T(8,128)}, u32[]{:S(2)}) copy-start(s32[256,256]{1,0:T(8,128)} %param.17) | copy-start | bytes 786436
  (37 other events, 100.5 us)
Sparse Core Ops, SparseCore 0:
  26.6 50.0 all-gather.4
  163.1 82.4 reduce-scatter.1
where the time goes:
time: 402 us; the launch traced here: 397 us
  blocking collectives  147 us (37%)
  waiting for transfers between devices  123 us (31%)
  matrix products  50.1 us (12%)
  other arithmetic  45.3 us (11%)
  between operations  18.3 us (5%)
  local copies, waits for them, and re-layouts  12.9 us (3%)
    reduce_scatter x1, waiting for transfers between devices, body(): lax.psum_scatter(jnp.einsum('bis,bjs->bij', part_above, part_below, preci...  80.7 us
    unnamed x1, blocking collectives  64.8 us
    psum x1, blocking collectives, body(): grad_exch, grad_omega = lax.psum((d_exch, d_omega), ('site', 'branch'))  64.7 us
    all_gather x1, waiting for transfers between devices, body(): probs = lax.all_gather(own_probs, 'site', axis=0, tiled=True)  41.9 us
    unnamed x13, other arithmetic  17.4 us
    dot_general x1, matrix products, body(): jnp.einsum('bis,bjs->bij', part_above, part_below, precision=lax.Precisio...  15.7 us
    dot_general x35, matrix products, product(): jnp.einsum('bij,bjk->bik', left, right, precision=lax.Precision.HIGHEST)  15.2 us
    dot_general x7, matrix products, forward(): jnp.einsum('bij,bjs->bis', probs, vectors, precision=lax.Precision.HIGHEST)  11.2 us
  transfers between devices with their start and end apart: 2, of which 2 were waited for; matrix products, arithmetic and copies ran while one was open for 2% of the time, Pallas kernels for 0%

commit v1 on v0

--- a/solution.py
+++ b/solution.py
@@ -146,7 +146,9 @@
     own_scaled = lax.dynamic_slice_in_dim(scaled, own_start, per_dev, 0)
     own_pull = None
     own_probs, own_pull = jax.vjp(expm_taylor, own_scaled)
-    probs = lax.all_gather(own_probs, "site", axis=0, tiled=True)
+    probs = jnp.concatenate(
+        lax.all_to_all(jnp.stack([own_probs] * lax.axis_size("site")), "site", 0, 0), axis=0
+    )
     taxon_rows = lax.dynamic_slice_in_dim(leaf_order, subtree * LEAF_DEV, LEAF_DEV, 0)
     leaves = leaf_partials(
         jnp.take(states, taxon_rows, axis=0), jnp.take(gap_mask, taxon_rows, axis=0)

time: 402 us -> 410 us (1.020)
  waiting for transfers between devices: 123 us -> 102 us
  local copies, waits for them, and re-layouts: 12.9 us -> 27.7 us
  starting transfers between devices: 0.61 us -> 10.2 us
  other arithmetic: 45.3 us -> 50.4 us
    all_gather x1 -> x0, waiting for transfers between devices: 41.9 us -> none  [body(): probs = lax.all_gather(own_probs, 'site', axis=0, tiled=True)]
    all_to_all x0 -> x1, waiting for transfers between devices: none -> 22.4 us  [body(): lax.all_to_all(jnp.stack([own_probs] * lax.axis_size('site')), 'site', 0, 0)]
    all_to_all x0 -> x1, starting transfers between devices: none -> 9.6 us  [body(): lax.all_to_all(jnp.stack([own_probs] * lax.axis_size('site')), 'site', 0, 0)]
    unnamed x171 -> x175, local copies, waits for them, and re-layouts: 8.97 us -> 17.3 us
    all_to_all x0 -> x1, other arithmetic: none -> 7.38 us  [body(): lax.all_to_all(jnp.stack([own_probs] * lax.axis_size('site')), 'site', 0, 0)]
  transfers between devices with their start and end apart: 2 -> 2, of which waited for: 2 -> 2; matrix products, arithmetic and copies ran while one was open for 2% -> 1% of each run, Pallas kernels for 0% -> 0%
where the time goes in v1:
time: 410 us; the launch traced here: 403 us
  blocking collectives  148 us (36%)
  waiting for transfers between devices  102 us (25%)
  other arithmetic  50.4 us (12%)
  matrix products  47.5 us (12%)
  local copies, waits for them, and re-layouts  27.7 us (7%)
  between operations  18.3 us (4%)
  starting transfers between devices  10.2 us (2%)
    reduce_scatter x1, waiting for transfers between devices, body(): lax.psum_scatter(jnp.einsum('bis,bjs->bij', part_above, part_below, preci...  79.3 us
    unnamed x1, blocking collectives  64.8 us
    psum x1, blocking collectives, body(): grad_exch, grad_omega = lax.psum((d_exch, d_omega), ('site', 'branch'))  64.6 us
    all_to_all x1, waiting for transfers between devices, body(): lax.all_to_all(jnp.stack([own_probs] * lax.axis_size('site')), 'site', 0, 0)  22.4 us
    unnamed x13, other arithmetic  17.6 us
    unnamed x175, local copies, waits for them, and re-layouts  17.3 us
    dot_general x1, matrix products, body(): jnp.einsum('bis,bjs->bij', part_above, part_below, precision=lax.Precisio...  15.7 us
    dot_general x35, matrix products, product(): jnp.einsum('bij,bjk->bik', left, right, precision=lax.Precision.HIGHEST)  14.5 us
  transfers between devices with their start and end apart: 2, of which 2 were waited for; matrix products, arithmetic and copies ran while one was open for 1% of the time, Pallas kernels for 0%

profile of v1, /device:TPU:1, one launch (start us, length us, event | category | flops | bytes accessed | tf_op | source)
XLA Modules:
  0.0 403.3 jit_solution(15843114779611618227)
XLA Ops:
  7.2 0.7 broadcast_add_fusion
  7.9 0.8 copy.99
  8.7 0.7 pad_add_fusion
  9.5 0.7 pad_maximum_fusion.5
  10.8 1.3 fusion.77
  12.8 0.8 fusion.62
  13.5 1.0 fusion.29
  14.6 2.7 fusion.27
  18.0 0.7 copy.144
  25.8 2.5 stack.40
  28.2 5.5 %reshape.344 = f32[32,1,16384]{2,1,0:T(1,128)} reshape(f32[32,4,64,64]{3,2,1,0:T(8,128)} %stack.40) | data formatting | bytes 4194304
  33.8 9.6 %all-to-all-start = ((f32[32,1,16384]{2,1,0:T(1,128)}), f32[32,1,16384]{2,1,0:T(1,128)S(1)}, u32[]{:S(2)}, u32[]{:S(2)}) async-start(f32[32,1,16384]{2,1,0:T(1,128)} %reshape.344), calls=%async_computation | async-start | bytes 4194304 | tf_op jit(solution)/shard_map/all_to_all | solution.py:150
  46.1 2.7 fusion.6
  48.8 22.4 %all-to-all-done = f32[32,1,16384]{2,1,0:T(1,128)S(1)} async-done(((f32[32,1,16384]{2,1,0:T(1,128)}), f32[32,1,16384]{2,1,0:T(1,128)S(1)}, u32[]{:S(2)}, u32[]{:S(2)}) %all-to-all-start) | async-done | bytes 2097184 | tf_op jit(solution)/shard_map/all_to_all | solution.py:150
  71.2 1.4 copy-done.6
  73.1 7.4 %reduce.5 = f32[32,16384]{1,0:T(8,128)S(1)} reduce(f32[32,1,16384]{2,1,0:T(1,128)} %copy-done.6, f32[]{:T(128)} %broadcast.256), dimensions={1}, to_apply=%all_to_all.3.reduce_sub_computation | reduce | bytes 4194308 | tf_op jit(solution)/shard_map/all_to_all | solution.py:150
  80.5 3.2 reshape.345
  83.7 1.1 slice.158
  84.8 1.1 slice.157
  85.9 1.3 slice.156
  87.3 4.6 %fusion.7 = f32[64,64,256]{2,1,0:T(8,128)S(1)} fusion(f32[64,64,64]{2,1,0:T(8,128)S(1)} %bitcast.207, s32[64,256]{1,0:T(8,128)S(1)} %broadcast_select_fusion, pred[64,256]{1,0:T(8,128)(4,1)S(1)} %select_compare_fusion), kind=kOutput, calls=%fused_computation.13 | convolution fusion | flops 808452096 | bytes 5324800 | tf_op jit(solution)/shard_map/bij,bjs->bis/dot_general | solution.py:55
  92.3 2.0 fusion.24
  94.6 1.1 fusion.26
  97.7 9.7 %all-gather = f32[256,256]{1,0:T(8,128)S(1)} all-gather(f32[64,256]{1,0:T(8,128)S(1)} %fusion.54), channel_id=2, replica_groups=mesh['site'=32,'branch'=4] {'branch'}, dimensions={0}, use_global_device_ids=true | all-gather | bytes 327680 | tf_op jit(solution)/shard_map/all_gather | solution.py:158
  109.8 8.4 %all-gather.2 = f32[4,1,256]{2,1,0:T(1,128)} all-gather(f32[1,1,256]{2,1,0:T(1,128)S(1)} %bitcast.220), channel_id=3, replica_groups=mesh['site'=32,'branch'=4] {'branch'}, dimensions={0}, use_global_device_ids=true | all-gather | bytes 5120 | tf_op jit(solution)/shard_map/all_gather | solution.py:159
  123.4 0.8 multiply_divide_fusion.2
  124.2 1.1 fusion.84
  125.3 1.0 fusion.12
  127.6 0.9 multiply_divide_fusion.1
  128.5 2.1 fusion.85
  130.6 1.9 fusion.11
  132.5 2.4 multiply_bitcast_fusion.1
  135.4 1.4 fusion.5
  136.9 3.6 constant_dynamic-update-slice_fusion.1
  140.5 1.2 reduce_sum.398
  141.8 3.4 multiply_dynamic-update-slice_fusion
  145.2 1.1 multiply_dynamic-update-slice_fusion.1
  146.3 0.8 multiply_dynamic-update-slice_fusion.2
  147.1 0.7 multiply_dynamic-update-slice_fusion.3
  150.4 1.2 fusion.25
  151.6 0.9 fusion.30
  152.5 0.7 fusion.44
  155.2 15.7 %fusion.86 = f32[128,64,64]{2,1,0:T(8,128)} fusion(f32[128,64,256]{2,1,0:T(8,128)} %constant_dynamic-update-slice_fusion, f32[128,64,256]{2,1,0:T(8,128)} %constant_dynamic-update-slice_fusion.2), kind=kOutput, calls=%fused_computation.226 | convolution fusion | flops 1610612736 | bytes 18874368 | tf_op jit(solution)/shard_map/bis,bjs->bij/dot_general | solution.py:174
  172.9 79.3 %reduce-scatter.2.cloned.1.call-done = f32[4,64,64]{2,1,0:T(8,128)} async-done(((f32[128,64,64]{2,1,0:T(8,128)}), f32[4,64,64]{2,1,0:T(8,128)}) %reduce-scatter.2.cloned.1.call-update) | async-done | bytes 65552 | tf_op jit(solution)/shard_map/reduce_scatter | solution.py:173
  252.2 1.3 fusion.87
  253.5 1.2 convolution_add_fusion.10
  265.0 64.8 %all-reduce.2 = (f32[128]{0:T(128)}, f32[]{:T(128)}) all-reduce(f32[128]{0:T(128)S(1)} %dynamic-update-slice, f32[]{:T(128)} %get-tuple-element.42), channel_id=1, replica_groups=mesh['site'=32,'branch'=4] {'site'}, use_global_device_ids=true, to_apply=%add | all-reduce | flops 129 | bytes 1032
  330.5 64.6 %all-reduce.1 = (f32[64,64]{1,0:T(8,128)}, f32[8]{0:T(128)}) all-reduce(f32[64,64]{1,0:T(8,128)S(1)} %fusion.61, f32[8]{0:T(128)S(1)} %get-tuple-element.5), channel_id=1, replica_groups=mesh['site'=32,'branch'=4] {'site','branch'}, use_global_device_ids=true, to_apply=%region_29.31 | all-reduce | flops 4104 | bytes 32832 | tf_op jit(solution)/shard_map/psum | solution.py:191
  (286 shorter events, 39.6 us)
Async XLA Ops:
  7.2 37.5 %copy-start = (s32[256,256]{1,0:T(8,128)S(1)}, s32[256,256]{1,0:T(8,128)}, u32[]{:S(2)}) copy-start(s32[256,256]{1,0:T(8,128)} %param.17) | copy-start | bytes 786436
  7.2 13.9 %copy-start.13 = (f32[64,64]{1,0:T(8,128)}, f32[64,64]{1,0:T(8,128)S(1)}, u32[]{:S(2)}) copy-start(f32[64,64]{1,0:T(8,128)S(1)} %fusion.63) | copy-start | bytes 49156
  7.9 9.5 %copy-start.70 = (f32[8]{0:T(128)}, f32[8]{0:T(128)S(1)}, u32[]{:S(2)}) copy-start(f32[8]{0:T(128)S(1)} %broadcast_add_fusion) | copy-start | bytes 100
  9.5 7.9 %copy-start.79 = (s32[128]{0:T(128)}, s32[128]{0:T(128)S(1)}, u32[]{:S(2)}) copy-start(s32[128]{0:T(128)S(1)} %pad_add_fusion) | copy-start | bytes 1540
  10.8 10.3 %copy-start.52 = (f32[4]{0:T(128)}, f32[4]{0:T(128)S(1)}, u32[]{:S(2)}) copy-start(f32[4]{0:T(128)S(1)} %get-tuple-element.14) | copy-start | bytes 52
  28.2 15.7 %copy-start.76 = (s32[256]{0:T(256)S(1)}, s32[256]{0:T(256)}, u32[]{:S(2)}) copy-start(s32[256]{0:T(256)} %param.19) | copy-start | bytes 3076
  28.2 16.3 %copy-start.82 = (s32[256]{0:T(256)S(1)}, s32[256]{0:T(256)}, u32[]{:S(2)}) copy-start(s32[256]{0:T(256)} %param.20) | copy-start | bytes 3076
  28.2 17.1 %copy-start.39 = (s32[256,256]{1,0:T(8,128)S(1)}, s32[256,256]{1,0:T(8,128)}, u32[]{:S(2)}) copy-start(s32[256,256]{1,0:T(8,128)} %param.18) | copy-start | bytes 786436
  33.8 37.5 %all-to-all-start = ((f32[32,1,16384]{2,1,0:T(1,128)}), f32[32,1,16384]{2,1,0:T(1,128)S(1)}, u32[]{:S(2)}, u32[]{:S(2)}) async-start(f32[32,1,16384]{2,1,0:T(1,128)} %reshape.344), calls=%async_computation | async-start | bytes 4194304 | tf_op jit(solution)/shard_map/all_to_all | solution.py:150
  43.4 208.8 %reduce-scatter.2.cloned.1.call-start = ((), (), s32[]{:S(2)}) async-start(), calls=%async_computation.2 | async-start | bytes 4325376 | tf_op jit(solution)/shard_map/reduce_scatter | solution.py:173
  95.7 11.8 %copy-start.62 = (f32[64]{0:T(128)S(1)}, f32[64]{0:T(128)}, u32[]{:S(2)}) copy-start(f32[64]{0:T(128)} %copy-done.61) | copy-start | bytes 772
  96.4 24.5 %copy-start.7 = (f32[8,64,256]{2,1,0:T(8,128)}, f32[8,64,256]{2,1,0:T(8,128)S(1)}, u32[]{:S(2)}) copy-start(f32[8,64,256]{2,1,0:T(8,128)S(1)} %fusion.31) | copy-start | bytes 1572868
  97.1 22.5 %copy-start.57 = (f32[256]{0:T(256)S(1)}, f32[256]{0:T(256)}, u32[]{:S(2)}) copy-start(f32[256]{0:T(256)} %convert_element_type.42) | copy-start | bytes 3076
  97.1 21.1 %copy-start.64 = (f32[2,256]{1,0:T(2,128)}, f32[2,256]{1,0:T(2,128)S(1)}, u32[]{:S(2)}) copy-start(f32[2,256]{1,0:T(2,128)S(1)} %fusion.71) | copy-start | bytes 6148
  97.5 22.1 %copy-start.23 = (f32[2,64,256]{2,1,0:T(8,128)}, f32[2,64,256]{2,1,0:T(8,128)S(1)}, u32[]{:S(2)}) copy-start(f32[2,64,256]{2,1,0:T(8,128)S(1)} %fusion.60) | copy-start | bytes 393220
  97.5 20.7 %copy-start.67 = (f32[256]{0:T(256)}, f32[256]{0:T(256)S(1)}, u32[]{:S(2)}) copy-start(f32[256]{0:T(256)S(1)} %fusion.70) | copy-start | bytes 3076
  109.4 9.2 %copy-start.40 = (f32[1,1,64,256]{3,2,1,0:T(8,128)}, f32[1,1,64,256]{3,2,1,0:T(8,128)S(1)}, u32[]{:S(2)}) copy-start(f32[1,1,64,256]{3,2,1,0:T(8,128)S(1)} %get-tuple-element.38) | copy-start | bytes 196612
  109.4 9.2 %copy-start.42 = (f32[1,1,64,256]{3,2,1,0:T(8,128)}, f32[1,1,64,256]{3,2,1,0:T(8,128)S(1)}, u32[]{:S(2)}) copy-start(f32[1,1,64,256]{3,2,1,0:T(8,128)S(1)} %get-tuple-element.39) | copy-start | bytes 196612
  141.8 6.7 %copy-start.74 = (f32[256]{0:T(256)S(1)}, f32[256]{0:T(256)}, u32[]{:S(2)}) copy-start(f32[256]{0:T(256)} %multiply_reduce_fusion.10) | copy-start | bytes 3076
  141.8 6.7 %copy-start.75 = (f32[256]{0:T(256)S(1)}, f32[256]{0:T(256)}, u32[]{:S(2)}) copy-start(f32[256]{0:T(256)} %get-tuple-element.15) | copy-start | bytes 3076
  141.8 6.7 %copy-start.77 = (s32[256]{0:T(256)S(1)}, s32[256]{0:T(256)}, u32[]{:S(2)}) copy-start(s32[256]{0:T(256)} %param.19) | copy-start | bytes 3076
  141.8 6.7 %copy-start.78 = (f32[256]{0:T(256)S(1)}, f32[256]{0:T(256)}, u32[]{:S(2)}) copy-start(f32[256]{0:T(256)} %reduce_sum.398) | copy-start | bytes 3076
  141.8 7.4 %copy-start.45 = (f32[1,64,256]{2,1,0:T(8,128)S(1)}, f32[1,64,256]{2,1,0:T(8,128)}, u32[]{:S(2)}) copy-start(f32[1,64,256]{2,1,0:T(8,128)} %copy-done.44) | copy-start | bytes 196612
  145.2 7.3 %copy-start.8 = (f32[8,64,256]{2,1,0:T(8,128)S(1)}, f32[8,64,256]{2,1,0:T(8,128)}, u32[]{:S(2)}) copy-start(f32[8,64,256]{2,1,0:T(8,128)} %copy-done.7) | copy-start | bytes 1572868
  145.2 7.3 %copy-start.59 = (f32[4,256]{1,0:T(4,128)S(1)}, f32[4,256]{1,0:T(4,128)}, u32[]{:S(2)}) copy-start(f32[4,256]{1,0:T(4,128)} %copy-done.58) | copy-start | bytes 12292
  146.3 7.0 %copy-start.65 = (f32[2,256]{1,0:T(2,128)S(1)}, f32[2,256]{1,0:T(2,128)}, u32[]{:S(2)}) copy-start(f32[2,256]{1,0:T(2,128)} %copy-done.64) | copy-start | bytes 6148
  146.3 7.6 %copy-start.24 = (f32[2,64,256]{2,1,0:T(8,128)S(1)}, f32[2,64,256]{2,1,0:T(8,128)}, u32[]{:S(2)}) copy-start(f32[2,64,256]{2,1,0:T(8,128)} %copy-done.23) | copy-start | bytes 393220
  146.3 7.6 %copy-start.68 = (f32[256]{0:T(256)S(1)}, f32[256]{0:T(256)}, u32[]{:S(2)}) copy-start(f32[256]{0:T(256)} %copy-done.67) | copy-start | bytes 3076
  170.8 81.3 %copy-start.20 = (f32[4,64,64]{2,1,0:T(8,128)S(1)}, f32[4,64,64]{2,1,0:T(8,128)}, u32[]{:S(2)}) copy-start(f32[4,64,64]{2,1,0:T(8,128)} %copy-done.19) | copy-start | bytes 196612
  170.9 83.9 %copy-start.18 = (f32[4,64,64]{2,1,0:T(8,128)S(1)}, f32[4,64,64]{2,1,0:T(8,128)}, u32[]{:S(2)}) copy-start(f32[4,64,64]{2,1,0:T(8,128)} %copy-done.17) | copy-start | bytes 196612
  170.9 84.6 %copy-start.16 = (f32[4,64,64]{2,1,0:T(8,128)S(1)}, f32[4,64,64]{2,1,0:T(8,128)}, u32[]{:S(2)}) copy-start(f32[4,64,64]{2,1,0:T(8,128)} %copy-done.15) | copy-start | bytes 196612
  170.9 85.5 %copy-start.22 = (f32[4,64,64]{2,1,0:T(8,128)S(1)}, f32[4,64,64]{2,1,0:T(8,128)}, u32[]{:S(2)}) copy-start(f32[4,64,64]{2,1,0:T(8,128)} %copy-done.21) | copy-start | bytes 196612
  170.9 86.4 %copy-start.26 = (f32[4,64,64]{2,1,0:T(8,128)S(1)}, f32[4,64,64]{2,1,0:T(8,128)}, u32[]{:S(2)}) copy-start(f32[4,64,64]{2,1,0:T(8,128)} %copy-done.25) | copy-start | bytes 196612
  170.9 86.7 %copy-start.53 = (f32[4]{0:T(128)S(1)}, f32[4]{0:T(128)}, u32[]{:S(2)}) copy-start(f32[4]{0:T(128)} %copy-done.52) | copy-start | bytes 52
  170.9 87.7 %copy-start.38 = (f32[4,64,64]{2,1,0:T(8,128)S(1)}, f32[4,64,64]{2,1,0:T(8,128)}, u32[]{:S(2)}) copy-start(f32[4,64,64]{2,1,0:T(8,128)} %copy-done.37) | copy-start | bytes 196612
  170.9 88.5 %copy-start.36 = (f32[4,64,64]{2,1,0:T(8,128)S(1)}, f32[4,64,64]{2,1,0:T(8,128)}, u32[]{:S(2)}) copy-start(f32[4,64,64]{2,1,0:T(8,128)} %copy-done.35) | copy-start | bytes 196612
  170.9 89.3 %copy-start.34 = (f32[4,64,64]{2,1,0:T(8,128)S(1)}, f32[4,64,64]{2,1,0:T(8,128)}, u32[]{:S(2)}) copy-start(f32[4,64,64]{2,1,0:T(8,128)} %copy-done.33) | copy-start | bytes 196612
  171.0 90.1 %copy-start.32 = (f32[4,64,64]{2,1,0:T(8,128)S(1)}, f32[4,64,64]{2,1,0:T(8,128)}, u32[]{:S(2)}) copy-start(f32[4,64,64]{2,1,0:T(8,128)} %copy-done.31) | copy-start | bytes 196612
  172.9 89.0 %copy-start.30 = (f32[4,64,64]{2,1,0:T(8,128)S(1)}, f32[4,64,64]{2,1,0:T(8,128)}, u32[]{:S(2)}) copy-start(f32[4,64,64]{2,1,0:T(8,128)} %copy-done.29) | copy-start | bytes 196612
  254.7 7.9 %copy-start.28 = (f32[4,64,64]{2,1,0:T(8,128)S(1)}, f32[4,64,64]{2,1,0:T(8,128)}, u32[]{:S(2)}) copy-start(f32[4,64,64]{2,1,0:T(8,128)} %copy-done.27) | copy-start | bytes 196612
  255.5 7.5 %copy-start.14 = (f32[64,64]{1,0:T(8,128)S(1)}, f32[64,64]{1,0:T(8,128)}, u32[]{:S(2)}) copy-start(f32[64,64]{1,0:T(8,128)} %copy-done.13) | copy-start | bytes 49156
  255.5 7.5 %copy-start.81 = (f32[4]{0:T(128)S(1)}, f32[4]{0:T(128)}, u32[]{:S(2)}) copy-start(f32[4]{0:T(128)} %get-tuple-element.13) | copy-start | bytes 52
  255.9 7.6 %copy-start.47 = (f32[64,64]{1,0:T(8,128)S(1)}, f32[64,64]{1,0:T(8,128)}, u32[]{:S(2)}) copy-start(f32[64,64]{1,0:T(8,128)} %copy-done.46) | copy-start | bytes 49156
  255.9 7.6 %copy-start.49 = (f32[8,64]{0,1:T(8,128)S(1)}, f32[8,64]{0,1:T(8,128)}, u32[]{:S(2)}) copy-start(f32[8,64]{0,1:T(8,128)} %copy-done.48) | copy-start | bytes 6148
  255.9 7.6 %copy-start.50 = (f32[64,64]{1,0:T(8,128)S(1)}, f32[64,64]{1,0:T(8,128)}, u32[]{:S(2)}) copy-start(f32[64,64]{1,0:T(8,128)} %constant.103) | copy-start | bytes 49156
  256.0 7.6 %copy-start.51 = (f32[64,64]{1,0:T(8,128)S(1)}, f32[64,64]{1,0:T(8,128)}, u32[]{:S(2)}) copy-start(f32[64,64]{1,0:T(8,128)} %constant.102) | copy-start | bytes 49156
  256.0 7.6 %copy-start.71 = (f32[8]{0:T(128)S(1)}, f32[8]{0:T(128)}, u32[]{:S(2)}) copy-start(f32[8]{0:T(128)} %copy-done.70) | copy-start | bytes 100
  258.1 137.0 %copy-start.1 = (s32[256,256]{1,0:T(8,128)S(1)}, s32[256,256]{1,0:T(8,128)}, u32[]{:S(2)}) copy-start(s32[256,256]{1,0:T(8,128)} %param.17) | copy-start | bytes 786436
  (39 other events, 118.0 us)
Sparse Core Ops, SparseCore 0:
  171.1 81.0 reduce-scatter.1
